TPU v7x, 32 devices: a whole 2x2x4 slice. The times are simulated.
32 devices in a mesh: sub: 8 (over z, y), grp: 4 (over x, core).
Axes of the slice: x: 2, y: 2, z: 4, core: 2. Of those that a mesh axis runs over, the one named last changes fastest.
Arguments:
- schur: bfloat16 [8, 2048, 2048], P('sub', 'grp'), may hold values from -0.125 to 0.125
- rhs: float32 [8, 2048, 192], P('sub', 'grp'), may hold values from -6 to 6
- start: float32 [8, 2048, 192], P('sub', 'grp'), may hold values from -6 to 6
- project: bfloat16 [8, 32, 4096], P('sub', 'grp'), may hold values from -0.75 to 0.75
- coarse_basis: bfloat16 [8, 8, 2048], P('sub', None, 'grp'), may hold values from -0.375 to 0.375
- owner_of_face: int32 [8, 32, 1], replicated, may hold values from 0 to 4; in each aligned block of 32 rows (0 to 31, 32 to 63, ..., all dimensions but the last counted through in order) at most 8 rows name the same one
- mortar_of_face: int32 [8, 32], replicated, may hold values from 0 to 15
- mortar_order: int32 [8, 16], replicated, may hold values from 3 to 7
- subdomain_map: int32 [8], replicated, may hold values from 0 to 7, each once
- vertex_ids: int32 [8, 8], replicated, may hold values from 0 to 15, all different within a row
Outputs:
- solution: float32 [8, 2048, 192], P('sub', 'grp')
Inputs may be any that keep to these rules, and one draw needn't show every extreme that they name: `owner_of_face`: the 32 faces of one subdomain name one offset at most 8 times. `mortar_of_face`: faces with the same owner and the same number lie on one mortar. `mortar_order`: row o holds the orders of the mortars owned by index o. `subdomain_map`: each subdomain once. `vertex_ids`: the 8 vertices of a subdomain differ; every vertex belongs to some subdomain.
All inputs are finite; a program needn't handle non-finite values.
Results may differ from a plain program's by a relative error of at most 0.0031.
Values may be sent and summed in bfloat16 or wider, within the bound.
No kernel may reach another device: no remote copies, remote signals or barrier semaphores. Data moves between devices by JAX's collectives and lax.ppermute only.
A program may use at most 64 MiB of HBM per device.

v0:
```python
import jax
import jax.numpy as jnp
from jax import lax
from jax.sharding import PartitionSpec as P

DEG = 8
FPTS = 64
MODES = 64
MORT_OWN = 16
ITERS = 2
REACH = 2
CAP = 8
relax_weight = 0.5
coarse_weight = 0.5


def passed_along(value, axis, steps):
    count = lax.axis_size(axis)
    pairs = [(source, (source + steps) % count) for source in range(count)]
    return lax.ppermute(value, axis, pairs)


def body(
    schur,
    rhs,
    start,
    project,
    coarse_basis,
    owner_of_face,
    mortar_of_face,
    mortar_order,
    subdomain_map,
    vertex_ids,
):
    highest = lax.Precision.HIGHEST
    contract_first = (((0,), (0,)), ((), ()))
    sub_count = lax.axis_size("sub")
    position = lax.axis_index("sub")
    all_faces = owner_of_face.shape[1]
    own_faces = project.shape[1]
    own_rows = schur.shape[1]
    neighbours = 2 * REACH + 1
    capacity = CAP
    vertices = 2 * sub_count
    held = jnp.take(owner_of_face[:, :, 0], subdomain_map, axis=0)
    mortar_local = jnp.take(mortar_of_face, subdomain_map, axis=0)
    face_index = jnp.arange(all_faces, dtype=jnp.int32)
    earlier = face_index[None, :] < face_index[:, None]
    ranks = jnp.sum(
        ((held[:, :, None] == held[:, None, :]) & earlier[None, :, :]).astype(jnp.int32), axis=2
    )
    my_held = lax.dynamic_index_in_dim(held, position, 0, keepdims=False)
    my_ranks = lax.dynamic_index_in_dim(ranks, position, 0, keepdims=False)
    slot_ids = my_held * capacity + my_ranks
    send_table = (
        jnp.arange(neighbours * capacity, dtype=jnp.int32)[:, None] == slot_ids[None, :]
    ).astype(jnp.bfloat16)
    links = jnp.arange(neighbours, dtype=jnp.int32)
    senders = jnp.mod(position - links + REACH, sub_count)
    from_held = jnp.take(held, senders, axis=0)
    from_mortar = jnp.take(mortar_local, senders, axis=0)
    from_ranks = jnp.take(ranks, senders, axis=0)
    incoming = (from_held == links[:, None]).astype(jnp.float32)
    mortar_hot = (
        from_mortar[:, :, None] == jnp.arange(MORT_OWN, dtype=jnp.int32)[None, None, :]
    ).astype(jnp.float32)
    rank_hot = (
        from_ranks[:, :, None] == jnp.arange(capacity, dtype=jnp.int32)[None, None, :]
    ).astype(jnp.float32)
    counts = jnp.einsum("jfk,jf->k", mortar_hot, incoming)
    degree = jnp.arange(MODES, dtype=jnp.int32)
    orders = lax.dynamic_index_in_dim(mortar_order, position, 0, keepdims=False)[:, None]
    keep_mask = ((degree[None, :] // DEG <= orders) & (degree[None, :] % DEG <= orders)).astype(
        jnp.float32
    )
    divisor = jnp.maximum(counts, 1.0)
    joined = jnp.einsum("jfk,jfc->kjc", mortar_hot * incoming[:, :, None], rank_hot)
    owner_table = joined.reshape(MORT_OWN, neighbours * capacity).astype(jnp.bfloat16)
    my_corners = lax.dynamic_index_in_dim(
        jnp.take(vertex_ids, subdomain_map, axis=0), position, 0, keepdims=False
    )
    corner_hot = (my_corners[:, None] == jnp.arange(vertices, dtype=jnp.int32)[None, :]).astype(
        jnp.float32
    )
    coarse_wide = coarse_basis[0].astype(jnp.float32)
    tables = project[0].reshape(own_faces, MODES, FPTS)
    matrix = schur[0]
    target = rhs[0]
    traces = start[0]
    for repeat in range(ITERS):
        trace_b = traces.astype(jnp.bfloat16)
        product = jnp.dot(
            matrix,
            lax.all_gather(trace_b, "grp", axis=0, tiled=True),
            preferred_element_type=jnp.float32,
        )
        residual = (product - target).astype(jnp.bfloat16)
        face_res = residual.reshape(own_faces, FPTS, -1)
        coeffs = jnp.einsum(
            "fmp,fpr->fmr", tables, face_res, preferred_element_type=jnp.float32
        ).astype(jnp.bfloat16)
        grouped = lax.all_to_all(coeffs, "grp", split_axis=2, concat_axis=0, tiled=True)
        part_rhs = grouped.shape[2]
        payload = grouped.reshape(all_faces, MODES * part_rhs)
        outgoing = jnp.dot(send_table, payload, preferred_element_type=jnp.float32).astype(
            jnp.bfloat16
        )
        blocks = outgoing.reshape(neighbours, capacity, -1)
        arrivals = []
        for link in range(neighbours):
            arrivals.append(passed_along(blocks[link], "sub", link - REACH))
        arrived = jnp.concatenate(arrivals, axis=0)
        mortar_sums = jnp.dot(owner_table, arrived, preferred_element_type=jnp.float32)
        shaped = mortar_sums.reshape(MORT_OWN, MODES, part_rhs) / divisor[:, None, None]
        shaped = shaped * keep_mask[:, :, None]
        averages = shaped.reshape(MORT_OWN, MODES * part_rhs).astype(jnp.bfloat16)
        replies = lax.dot_general(
            owner_table, averages, contract_first, preferred_element_type=jnp.float32
        ).astype(jnp.bfloat16)
        reply_blocks = replies.reshape(neighbours, capacity, -1)
        answers = []
        for link in range(neighbours):
            answers.append(passed_along(reply_blocks[link], "sub", REACH - link))
        answered = jnp.concatenate(answers, axis=0)
        own_back = lax.dot_general(
            send_table, answered, contract_first, preferred_element_type=jnp.float32
        ).astype(jnp.bfloat16)
        returned = lax.all_to_all(
            own_back.reshape(all_faces, MODES, part_rhs),
            "grp",
            split_axis=0,
            concat_axis=2,
            tiled=True,
        )
        lifted = jnp.einsum(
            "fmp,fmr->fpr", tables, returned, preferred_element_type=jnp.float32
        ).reshape(own_rows, -1)
        partial_value = jnp.dot(coarse_wide, lifted, precision=highest)
        spread = lax.dot_general(corner_hot, partial_value, contract_first, precision=highest)
        vertex = lax.psum(spread, ("sub", "grp"))
        picked = jnp.dot(corner_hot, vertex, precision=highest)
        coarse_corr = lax.dot_general(coarse_wide, picked, contract_first, precision=highest)
        traces = traces - relax_weight * lifted - coarse_weight * coarse_corr
    return traces[None]


def solution(mesh):
    return jax.shard_map(
        body,
        mesh=mesh,
        in_specs=(
            P("sub", "grp", None),
            P("sub", "grp", None),
            P("sub", "grp", None),
            P("sub", "grp", None),
            P("sub", None, "grp"),
            P(),
            P(),
            P(),
            P(),
            P(),
        ),
        out_specs=P("sub", "grp", None),
        check_vma=False,
    )
```

profile of v0, /device:TPU:10, one launch (start us, length us, event | category | flops | bytes accessed | tf_op | source)
XLA Modules:
  0.0 199.1 jit_solution(15513312980948887110)
XLA Ops:
  0.0 1.2 reshape_squeeze.3
  1.2 1.0 bitcast_convert_fusion
  2.2 8.2 %all_gather.6 = bf16[2048,192]{0,1:T(8,128)(2,1)S(1)} all-gather(bf16[512,192]{0,1:T(8,128)(2,1)S(1)} %bitcast_convert_fusion), channel_id=1, replica_groups=mesh['sub'=8,'grp'=4] {'grp'}, dimensions={0}, use_global_device_ids=true | all-gather | bytes 983040 | tf_op jit(solution)/shard_map/all_gather | solution.py:94
  10.4 1.8 fusion.20
  12.9 1.0 reshape.310
  13.9 4.3 %all-to-all-start = ((bf16[4,2,12288]{2,1,0:T(2,128)(2,1)}), bf16[4,2,12288]{2,1,0:T(2,128)(2,1)S(1)}, u32[]{:S(2)}, u32[]{:S(2)}) async-start(bf16[4,2,12288]{2,1,0:T(2,128)(2,1)} %reshape.310), calls=%async_computation | async-start | bytes 393216 | tf_op jit(solution)/shard_map/all_to_all | solution.py:102
  18.3 0.6 gather_fusion.3
  18.9 0.6 gather_fusion.1
  19.5 0.3 convert_reduce_fusion
  19.8 0.6 gather_fusion.5
  20.4 0.6 gather_fusion.2
  20.9 0.6 gather_fusion.4
  21.5 0.7 fusion.62
  22.5 0.3 reshape.311
  22.8 0.3 copy.70
  23.2 0.8 reshape.235
  24.2 0.5 collective-permute-start
  24.8 1.6 collective-permute-start.4
  26.4 1.5 collective-permute-start.3
  27.9 1.6 collective-permute-start.1
  29.5 2.9 %collective-permute-done.1 = bf16[8,3072]{1,0:T(8,128)(2,1)S(1)} collective-permute-done((bf16[8,3072]{1,0:T(8,128)(2,1)S(1)}, bf16[8,3072]{1,0:T(8,128)(2,1)S(1)}, u32[]{:S(2)}, u32[]{:S(2)}) %collective-permute-start.1) | collective-permute-done | bytes 49184 | tf_op jit(solution)/shard_map/ppermute | solution.py:20
  32.4 0.7 collective-permute-done.3
  33.1 0.7 dot_general.91
  33.8 0.3 copy.72
  34.7 0.3 convert_element_type.96
  35.3 1.9 collective-permute-start.5
  37.2 0.6 gather_fusion
  37.7 0.9 collective-permute-start.9
  38.7 4.3 %collective-permute-start.8 = (bf16[8,3072]{1,0:T(8,128)(2,1)S(1)}, bf16[8,3072]{1,0:T(8,128)(2,1)S(1)}, u32[]{:S(2)}, u32[]{:S(2)}) collective-permute-start(bf16[8,3072]{1,0:T(8,128)(2,1)S(1)} %get-tuple-element.20), channel_id=1, source_target_pairs={{0,28},{4,0},{8,4},{12,8},{16,12},{20,16},{24,20},{28,24},{1,29},{... | collective-permute-start | bytes 147464 | tf_op jit(solution)/shard_map/ppermute | solution.py:20
  43.0 5.0 %collective-permute-done.6 = bf16[8,3072]{1,0:T(8,128)(2,1)S(1)} collective-permute-done((bf16[8,3072]{1,0:T(8,128)(2,1)S(1)}, bf16[8,3072]{1,0:T(8,128)(2,1)S(1)}, u32[]{:S(2)}, u32[]{:S(2)}) %collective-permute-start.6) | collective-permute-done | bytes 49184 | tf_op jit(solution)/shard_map/ppermute | solution.py:20
  48.3 0.5 reshape.236
  49.1 1.0 reshape.312
  50.1 4.3 %all-to-all-start.1 = ((bf16[4,2,12288]{2,1,0:T(2,128)(2,1)}), bf16[4,2,12288]{2,1,0:T(2,128)(2,1)S(1)}, u32[]{:S(2)}, u32[]{:S(2)}) async-start(bf16[4,2,12288]{2,1,0:T(2,128)(2,1)} %reshape.312), calls=%async_computation.1 | async-start | bytes 393216 | tf_op jit(solution)/shard_map/all_to_all | solution.py:128
  54.4 0.8 broadcast_select_fusion.4
  55.1 2.9 %all-to-all-done.1 = bf16[4,2,12288]{2,1,0:T(2,128)(2,1)S(1)} async-done(((bf16[4,2,12288]{2,1,0:T(2,128)(2,1)}), bf16[4,2,12288]{2,1,0:T(2,128)(2,1)S(1)}, u32[]{:S(2)}, u32[]{:S(2)}) %all-to-all-start.1) | async-done | bytes 196640 | tf_op jit(solution)/shard_map/all_to_all | solution.py:128
  58.0 0.3 reshape.313
  58.4 0.4 fusion.73
  59.2 0.3 fusion.55
  59.5 43.4 %psum.14 = f32[16,192]{1,0:T(8,128)S(1)} all-reduce(f32[16,192]{1,0:T(8,128)S(1)} %fusion.55), channel_id=1, replica_groups=mesh['sub'=8,'grp'=4] {'sub','grp'}, use_global_device_ids=true, to_apply=%region_1.0 | all-reduce | flops 3072 | bytes 24576 | tf_op jit(solution)/shard_map/psum | solution.py:140
  103.1 1.1 fusion.72
  104.2 7.2 %all_gather.7 = bf16[2048,192]{0,1:T(8,128)(2,1)S(1)} all-gather(bf16[512,192]{0,1:T(8,128)(2,1)S(1)} %get-tuple-element.33), channel_id=1, replica_groups=mesh['sub'=8,'grp'=4] {'grp'}, dimensions={0}, use_global_device_ids=true | all-gather | bytes 983040 | tf_op jit(solution)/shard_map/all_gather | solution.py:94
  111.4 0.8 fusion.23
  112.9 0.3 reshape.314
  113.2 8.0 %all_to_all.66 = bf16[4,2,12288]{2,1,0:T(2,128)(2,1)S(1)} all-to-all(bf16[4,2,12288]{2,1,0:T(2,128)(2,1)S(1)} %reshape.314), channel_id=1, replica_groups=mesh['sub'=8,'grp'=4] {'grp'}, dimensions={0} | all-to-all | bytes 393216 | tf_op jit(solution)/shard_map/all_to_all | solution.py:102
  121.2 0.3 reshape.315
  121.5 0.3 copy.82
  121.8 0.8 reshape.239
  122.9 2.0 %collective-permute-start.14 = (bf16[8,3072]{1,0:T(8,128)(2,1)S(1)}, bf16[8,3072]{1,0:T(8,128)(2,1)S(1)}, u32[]{:S(2)}, u32[]{:S(2)}) collective-permute-start(bf16[8,3072]{1,0:T(8,128)(2,1)S(1)} %get-tuple-element.14), channel_id=1, source_target_pairs={{0,8},{4,12},{8,16},{12,20},{16,24},{20,28},{24,0},{28,4},{1,9},{5... | collective-permute-start | bytes 147464 | tf_op jit(solution)/shard_map/ppermute | solution.py:20
  124.9 0.7 collective-permute-start.13
  125.7 2.2 %collective-permute-start.11 = (bf16[8,3072]{1,0:T(8,128)(2,1)S(1)}, bf16[8,3072]{1,0:T(8,128)(2,1)S(1)}, u32[]{:S(2)}, u32[]{:S(2)}) collective-permute-start(bf16[8,3072]{1,0:T(8,128)(2,1)S(1)} %get-tuple-element.17), channel_id=1, source_target_pairs={{0,28},{4,0},{8,4},{12,8},{16,12},{20,16},{24,20},{28,24},{1,29},{... | collective-permute-start | bytes 147464 | tf_op jit(solution)/shard_map/ppermute | solution.py:20
  127.9 2.4 %collective-permute-done.11 = bf16[8,3072]{1,0:T(8,128)(2,1)S(1)} collective-permute-done((bf16[8,3072]{1,0:T(8,128)(2,1)S(1)}, bf16[8,3072]{1,0:T(8,128)(2,1)S(1)}, u32[]{:S(2)}, u32[]{:S(2)}) %collective-permute-start.11) | collective-permute-done | bytes 49184 | tf_op jit(solution)/shard_map/ppermute | solution.py:20
  130.4 0.7 dot_general.107
  131.1 0.3 copy.84
  131.9 0.3 convert_element_type.105
  132.5 0.9 collective-permute-start.15
  133.4 1.2 collective-permute-start.19
  134.6 4.4 %collective-permute-start.18 = (bf16[8,3072]{1,0:T(8,128)(2,1)S(1)}, bf16[8,3072]{1,0:T(8,128)(2,1)S(1)}, u32[]{:S(2)}, u32[]{:S(2)}) collective-permute-start(bf16[8,3072]{1,0:T(8,128)(2,1)S(1)} %get-tuple-element.10), channel_id=1, source_target_pairs={{0,28},{4,0},{8,4},{12,8},{16,12},{20,16},{24,20},{28,24},{1,29},{... | collective-permute-start | bytes 147464 | tf_op jit(solution)/shard_map/ppermute | solution.py:20
  139.0 5.0 %collective-permute-done.16 = bf16[8,3072]{1,0:T(8,128)(2,1)S(1)} collective-permute-done((bf16[8,3072]{1,0:T(8,128)(2,1)S(1)}, bf16[8,3072]{1,0:T(8,128)(2,1)S(1)}, u32[]{:S(2)}, u32[]{:S(2)}) %collective-permute-start.16) | collective-permute-done | bytes 49184 | tf_op jit(solution)/shard_map/ppermute | solution.py:20
  144.3 0.5 reshape.240
  145.1 0.3 reshape.316
  145.4 7.6 %all_to_all.67 = bf16[4,2,12288]{2,1,0:T(2,128)(2,1)S(1)} all-to-all(bf16[4,2,12288]{2,1,0:T(2,128)(2,1)S(1)} %reshape.316), channel_id=1, replica_groups=mesh['sub'=8,'grp'=4] {'grp'}, dimensions={0} | all-to-all | bytes 393216 | tf_op jit(solution)/shard_map/all_to_all | solution.py:128
  153.4 0.4 fusion.74
  154.5 43.3 %psum.15 = f32[16,192]{1,0:T(8,128)S(1)} all-reduce(f32[16,192]{1,0:T(8,128)S(1)} %fusion.53), channel_id=1, replica_groups=mesh['sub'=8,'grp'=4] {'sub','grp'}, use_global_device_ids=true, to_apply=%region_2.5 | all-reduce | flops 3072 | bytes 24576 | tf_op jit(solution)/shard_map/psum | solution.py:140
  197.9 1.1 fusion.6
  (122 shorter events, 6.8 us)
Async XLA Ops:
  0.0 10.4 %copy-start = (bf16[1,512,2048]{2,1,0:T(8,128)(2,1)S(1)}, bf16[1,512,2048]{2,1,0:T(8,128)(2,1)}, u32[]{:S(2)}) copy-start(bf16[1,512,2048]{2,1,0:T(8,128)(2,1)} %param.14) | copy-start | bytes 6291460
  12.3 5.9 %copy-start.13 = (s32[8]{0:T(128)S(1)}, s32[8]{0:T(128)}, u32[]{:S(2)}) copy-start(s32[8]{0:T(128)} %param.22) | copy-start | bytes 100
  12.3 6.0 %copy-start.4 = (s32[8,32]{1,0:T(8,128)S(1)}, s32[8,32]{1,0:T(8,128)}, u32[]{:S(2)}) copy-start(s32[8,32]{1,0:T(8,128)} %param.20) | copy-start | bytes 3076
  12.3 6.6 %copy-start.5 = (s32[8,32,1]{1,2,0:T(1,128)S(1)}, s32[8,32,1]{1,2,0:T(1,128)}, u32[]{:S(2)}) copy-start(s32[8,32,1]{1,2,0:T(1,128)} %param.19) | copy-start | bytes 3076
  13.9 8.7 %all-to-all-start = ((bf16[4,2,12288]{2,1,0:T(2,128)(2,1)}), bf16[4,2,12288]{2,1,0:T(2,128)(2,1)S(1)}, u32[]{:S(2)}, u32[]{:S(2)}) async-start(bf16[4,2,12288]{2,1,0:T(2,128)(2,1)} %reshape.310), calls=%async_computation | async-start | bytes 393216 | tf_op jit(solution)/shard_map/all_to_all | solution.py:102
  18.2 4.6 %copy-start.12 = (pred[8]{0:T(512)(128)(4,1)}, pred[8]{0:T(512)(128)(4,1)S(1)}, u32[]{:S(2)}) copy-start(pred[8]{0:T(512)(128)(4,1)S(1)} %compare_and_fusion.1) | copy-start | bytes 28
  22.4 12.6 %copy-start.8 = (bf16[5,8,16]{2,1,0:T(8,128)(2,1)}, bf16[5,8,16]{2,1,0:T(8,128)(2,1)S(1)}, u32[]{:S(2)}) copy-start(bf16[5,8,16]{2,1,0:T(8,128)(2,1)S(1)} %convolution_convert_fusion.8) | copy-start | bytes 3844
  22.5 11.6 %copy-start.10 = (f32[16,64]{1,0:T(8,128)}, f32[16,64]{1,0:T(8,128)S(1)}, u32[]{:S(2)}) copy-start(f32[16,64]{1,0:T(8,128)S(1)} %and_convert_fusion) | copy-start | bytes 12292
  24.2 5.3 %collective-permute-start = (bf16[8,3072]{1,0:T(8,128)(2,1)S(1)}, bf16[8,3072]{1,0:T(8,128)(2,1)S(1)}, u32[]{:S(2)}, u32[]{:S(2)}) collective-permute-start(bf16[8,3072]{1,0:T(8,128)(2,1)S(1)} %get-tuple-element.28), channel_id=1, source_target_pairs={{0,24},{4,28},{8,0},{12,4},{16,8},{20,12},{24,16},{28,20},{1,25},{... | collective-permute-start | bytes 147464 | tf_op jit(solution)/shard_map/ppermute | solution.py:20
  24.8 9.9 %copy-start.14 = (f32[16]{0:T(128)}, f32[16]{0:T(128)S(1)}, u32[]{:S(2)}) copy-start(f32[16]{0:T(128)S(1)} %fusion.30) | copy-start | bytes 196
  24.8 8.3 %collective-permute-start.4 = (bf16[8,3072]{1,0:T(8,128)(2,1)S(1)}, bf16[8,3072]{1,0:T(8,128)(2,1)S(1)}, u32[]{:S(2)}, u32[]{:S(2)}) collective-permute-start(bf16[8,3072]{1,0:T(8,128)(2,1)S(1)} %get-tuple-element.24), channel_id=1, source_target_pairs={{0,8},{4,12},{8,16},{12,20},{16,24},{20,28},{24,0},{28,4},{1,9},{5... | collective-permute-start | bytes 147464 | tf_op jit(solution)/shard_map/ppermute | solution.py:20
  26.4 6.7 %collective-permute-start.3 = (bf16[8,3072]{1,0:T(8,128)(2,1)S(1)}, bf16[8,3072]{1,0:T(8,128)(2,1)S(1)}, u32[]{:S(2)}, u32[]{:S(2)}) collective-permute-start(bf16[8,3072]{1,0:T(8,128)(2,1)S(1)} %get-tuple-element.25), channel_id=1, source_target_pairs={{0,4},{4,8},{8,12},{12,16},{16,20},{20,24},{24,28},{28,0},{1,5},{5... | collective-permute-start | bytes 147464 | tf_op jit(solution)/shard_map/ppermute | solution.py:20
  27.9 4.5 %collective-permute-start.2 = (bf16[8,3072]{1,0:T(8,128)(2,1)S(1)}, bf16[8,3072]{1,0:T(8,128)(2,1)S(1)}, u32[]{:S(2)}, u32[]{:S(2)}) collective-permute-start(bf16[8,3072]{1,0:T(8,128)(2,1)S(1)} %get-tuple-element.26), channel_id=1, source_target_pairs={{0,0},{4,4},{8,8},{12,12},{16,16},{20,20},{24,24},{28,28},{1,1},{5... | collective-permute-start | bytes 147464 | tf_op jit(solution)/shard_map/ppermute | solution.py:20
  27.9 4.5 %collective-permute-start.1 = (bf16[8,3072]{1,0:T(8,128)(2,1)S(1)}, bf16[8,3072]{1,0:T(8,128)(2,1)S(1)}, u32[]{:S(2)}, u32[]{:S(2)}) collective-permute-start(bf16[8,3072]{1,0:T(8,128)(2,1)S(1)} %get-tuple-element.27), channel_id=1, source_target_pairs={{0,28},{4,0},{8,4},{12,8},{16,12},{20,16},{24,20},{28,24},{1,29},{... | collective-permute-start | bytes 147464 | tf_op jit(solution)/shard_map/ppermute | solution.py:20
  33.8 3.3 %copy-start.6 = (s32[8,8]{1,0:T(8,128)S(1)}, s32[8,8]{1,0:T(8,128)}, u32[]{:S(2)}) copy-start(s32[8,8]{1,0:T(8,128)} %param.23) | copy-start | bytes 772
  35.3 7.7 %collective-permute-start.5 = (bf16[8,3072]{1,0:T(8,128)(2,1)S(1)}, bf16[8,3072]{1,0:T(8,128)(2,1)S(1)}, u32[]{:S(2)}, u32[]{:S(2)}) collective-permute-start(bf16[8,3072]{1,0:T(8,128)(2,1)S(1)} %get-tuple-element.23), channel_id=1, source_target_pairs={{0,8},{4,12},{8,16},{12,20},{16,24},{20,28},{24,0},{28,4},{1,9},{5... | collective-permute-start | bytes 147464 | tf_op jit(solution)/shard_map/ppermute | solution.py:20
  37.7 10.3 %collective-permute-start.9 = (bf16[8,3072]{1,0:T(8,128)(2,1)S(1)}, bf16[8,3072]{1,0:T(8,128)(2,1)S(1)}, u32[]{:S(2)}, u32[]{:S(2)}) collective-permute-start(bf16[8,3072]{1,0:T(8,128)(2,1)S(1)} %get-tuple-element.19), channel_id=1, source_target_pairs={{0,24},{4,28},{8,0},{12,4},{16,8},{20,12},{24,16},{28,20},{1,25},{... | collective-permute-start | bytes 147464 | tf_op jit(solution)/shard_map/ppermute | solution.py:20
  38.7 9.3 %collective-permute-start.8 = (bf16[8,3072]{1,0:T(8,128)(2,1)S(1)}, bf16[8,3072]{1,0:T(8,128)(2,1)S(1)}, u32[]{:S(2)}, u32[]{:S(2)}) collective-permute-start(bf16[8,3072]{1,0:T(8,128)(2,1)S(1)} %get-tuple-element.20), channel_id=1, source_target_pairs={{0,28},{4,0},{8,4},{12,8},{16,12},{20,16},{24,20},{28,24},{1,29},{... | collective-permute-start | bytes 147464 | tf_op jit(solution)/shard_map/ppermute | solution.py:20
  43.0 5.0 %collective-permute-start.7 = (bf16[8,3072]{1,0:T(8,128)(2,1)S(1)}, bf16[8,3072]{1,0:T(8,128)(2,1)S(1)}, u32[]{:S(2)}, u32[]{:S(2)}) collective-permute-start(bf16[8,3072]{1,0:T(8,128)(2,1)S(1)} %get-tuple-element.21), channel_id=1, source_target_pairs={{0,0},{4,4},{8,8},{12,12},{16,16},{20,20},{24,24},{28,28},{1,1},{5... | collective-permute-start | bytes 147464 | tf_op jit(solution)/shard_map/ppermute | solution.py:20
  43.0 5.0 %collective-permute-start.6 = (bf16[8,3072]{1,0:T(8,128)(2,1)S(1)}, bf16[8,3072]{1,0:T(8,128)(2,1)S(1)}, u32[]{:S(2)}, u32[]{:S(2)}) collective-permute-start(bf16[8,3072]{1,0:T(8,128)(2,1)S(1)} %get-tuple-element.22), channel_id=1, source_target_pairs={{0,4},{4,8},{8,12},{12,16},{16,20},{20,24},{24,28},{28,0},{1,5},{5... | collective-permute-start | bytes 147464 | tf_op jit(solution)/shard_map/ppermute | solution.py:20
  49.1 9.8 %copy-start.7 = (bf16[1,8,512]{2,1,0:T(8,128)(2,1)S(1)}, bf16[1,8,512]{2,1,0:T(8,128)(2,1)}, u32[]{:S(2)}) copy-start(bf16[1,8,512]{2,1,0:T(8,128)(2,1)} %param.18) | copy-start | bytes 24580
  50.1 7.9 %all-to-all-start.1 = ((bf16[4,2,12288]{2,1,0:T(2,128)(2,1)}), bf16[4,2,12288]{2,1,0:T(2,128)(2,1)S(1)}, u32[]{:S(2)}, u32[]{:S(2)}) async-start(bf16[4,2,12288]{2,1,0:T(2,128)(2,1)} %reshape.312), calls=%async_computation.1 | async-start | bytes 393216 | tf_op jit(solution)/shard_map/all_to_all | solution.py:128
  54.4 48.7 %copy-start.1 = (f32[1,512,192]{1,2,0:T(8,128)S(1)}, f32[1,512,192]{1,2,0:T(8,128)}, u32[]{:S(2)}) copy-start(f32[1,512,192]{1,2,0:T(8,128)} %param.16) | copy-start | bytes 1179652
  102.9 8.5 %copy-start.3 = (f32[1,512,192]{1,2,0:T(8,128)S(1)}, f32[1,512,192]{1,2,0:T(8,128)}, u32[]{:S(2)}) copy-start(f32[1,512,192]{1,2,0:T(8,128)} %param.15) | copy-start | bytes 1179652
  121.8 9.6 %copy-start.9 = (bf16[5,8,16]{2,1,0:T(8,128)(2,1)S(1)}, bf16[5,8,16]{2,1,0:T(8,128)(2,1)}, u32[]{:S(2)}) copy-start(bf16[5,8,16]{2,1,0:T(8,128)(2,1)} %copy-done.8) | copy-start | bytes 3844
  121.8 9.6 %copy-start.11 = (f32[16,64]{1,0:T(8,128)S(1)}, f32[16,64]{1,0:T(8,128)}, u32[]{:S(2)}) copy-start(f32[16,64]{1,0:T(8,128)} %copy-done.10) | copy-start | bytes 12292
  121.8 9.6 %copy-start.15 = (f32[16]{0:T(128)S(1)}, f32[16]{0:T(128)}, u32[]{:S(2)}) copy-start(f32[16]{0:T(128)} %copy-done.14) | copy-start | bytes 196
  122.9 5.0 %collective-permute-start.10 = (bf16[8,3072]{1,0:T(8,128)(2,1)S(1)}, bf16[8,3072]{1,0:T(8,128)(2,1)S(1)}, u32[]{:S(2)}, u32[]{:S(2)}) collective-permute-start(bf16[8,3072]{1,0:T(8,128)(2,1)S(1)} %get-tuple-element.18), channel_id=1, source_target_pairs={{0,24},{4,28},{8,0},{12,4},{16,8},{20,12},{24,16},{28,20},{1,25},{... | collective-permute-start | bytes 147464 | tf_op jit(solution)/shard_map/ppermute | solution.py:20
  122.9 7.4 %collective-permute-start.14 = (bf16[8,3072]{1,0:T(8,128)(2,1)S(1)}, bf16[8,3072]{1,0:T(8,128)(2,1)S(1)}, u32[]{:S(2)}, u32[]{:S(2)}) collective-permute-start(bf16[8,3072]{1,0:T(8,128)(2,1)S(1)} %get-tuple-element.14), channel_id=1, source_target_pairs={{0,8},{4,12},{8,16},{12,20},{16,24},{20,28},{24,0},{28,4},{1,9},{5... | collective-permute-start | bytes 147464 | tf_op jit(solution)/shard_map/ppermute | solution.py:20
  124.9 5.4 %collective-permute-start.13 = (bf16[8,3072]{1,0:T(8,128)(2,1)S(1)}, bf16[8,3072]{1,0:T(8,128)(2,1)S(1)}, u32[]{:S(2)}, u32[]{:S(2)}) collective-permute-start(bf16[8,3072]{1,0:T(8,128)(2,1)S(1)} %get-tuple-element.15), channel_id=1, source_target_pairs={{0,4},{4,8},{8,12},{12,16},{16,20},{20,24},{24,28},{28,0},{1,5},{5... | collective-permute-start | bytes 147464 | tf_op jit(solution)/shard_map/ppermute | solution.py:20
  125.7 4.6 %collective-permute-start.12 = (bf16[8,3072]{1,0:T(8,128)(2,1)S(1)}, bf16[8,3072]{1,0:T(8,128)(2,1)S(1)}, u32[]{:S(2)}, u32[]{:S(2)}) collective-permute-start(bf16[8,3072]{1,0:T(8,128)(2,1)S(1)} %get-tuple-element.16), channel_id=1, source_target_pairs={{0,0},{4,4},{8,8},{12,12},{16,16},{20,20},{24,24},{28,28},{1,1},{5... | collective-permute-start | bytes 147464 | tf_op jit(solution)/shard_map/ppermute | solution.py:20
  125.7 4.6 %collective-permute-start.11 = (bf16[8,3072]{1,0:T(8,128)(2,1)S(1)}, bf16[8,3072]{1,0:T(8,128)(2,1)S(1)}, u32[]{:S(2)}, u32[]{:S(2)}) collective-permute-start(bf16[8,3072]{1,0:T(8,128)(2,1)S(1)} %get-tuple-element.17), channel_id=1, source_target_pairs={{0,28},{4,0},{8,4},{12,8},{16,12},{20,16},{24,20},{28,24},{1,29},{... | collective-permute-start | bytes 147464 | tf_op jit(solution)/shard_map/ppermute | solution.py:20
  132.5 6.5 %collective-permute-start.15 = (bf16[8,3072]{1,0:T(8,128)(2,1)S(1)}, bf16[8,3072]{1,0:T(8,128)(2,1)S(1)}, u32[]{:S(2)}, u32[]{:S(2)}) collective-permute-start(bf16[8,3072]{1,0:T(8,128)(2,1)S(1)} %get-tuple-element.13), channel_id=1, source_target_pairs={{0,8},{4,12},{8,16},{12,20},{16,24},{20,28},{24,0},{28,4},{1,9},{5... | collective-permute-start | bytes 147464 | tf_op jit(solution)/shard_map/ppermute | solution.py:20
  133.4 10.6 %collective-permute-start.19 = (bf16[8,3072]{1,0:T(8,128)(2,1)S(1)}, bf16[8,3072]{1,0:T(8,128)(2,1)S(1)}, u32[]{:S(2)}, u32[]{:S(2)}) collective-permute-start(bf16[8,3072]{1,0:T(8,128)(2,1)S(1)} %get-tuple-element.9), channel_id=1, source_target_pairs={{0,24},{4,28},{8,0},{12,4},{16,8},{20,12},{24,16},{28,20},{1,25},{... | collective-permute-start | bytes 147464 | tf_op jit(solution)/shard_map/ppermute | solution.py:20
  134.6 9.4 %collective-permute-start.18 = (bf16[8,3072]{1,0:T(8,128)(2,1)S(1)}, bf16[8,3072]{1,0:T(8,128)(2,1)S(1)}, u32[]{:S(2)}, u32[]{:S(2)}) collective-permute-start(bf16[8,3072]{1,0:T(8,128)(2,1)S(1)} %get-tuple-element.10), channel_id=1, source_target_pairs={{0,28},{4,0},{8,4},{12,8},{16,12},{20,16},{24,20},{28,24},{1,29},{... | collective-permute-start | bytes 147464 | tf_op jit(solution)/shard_map/ppermute | solution.py:20
  138.9 5.0 %collective-permute-start.17 = (bf16[8,3072]{1,0:T(8,128)(2,1)S(1)}, bf16[8,3072]{1,0:T(8,128)(2,1)S(1)}, u32[]{:S(2)}, u32[]{:S(2)}) collective-permute-start(bf16[8,3072]{1,0:T(8,128)(2,1)S(1)} %get-tuple-element.11), channel_id=1, source_target_pairs={{0,0},{4,4},{8,8},{12,12},{16,16},{20,20},{24,24},{28,28},{1,1},{5... | collective-permute-start | bytes 147464 | tf_op jit(solution)/shard_map/ppermute | solution.py:20
  138.9 5.0 %collective-permute-start.16 = (bf16[8,3072]{1,0:T(8,128)(2,1)S(1)}, bf16[8,3072]{1,0:T(8,128)(2,1)S(1)}, u32[]{:S(2)}, u32[]{:S(2)}) collective-permute-start(bf16[8,3072]{1,0:T(8,128)(2,1)S(1)} %get-tuple-element.12), channel_id=1, source_target_pairs={{0,4},{4,8},{8,12},{12,16},{16,20},{20,24},{24,28},{28,0},{1,5},{5... | collective-permute-start | bytes 147464 | tf_op jit(solution)/shard_map/ppermute | solution.py:20
  153.0 44.9 %copy-start.2 = (f32[512,192]{0,1:T(8,128)S(1)}, f32[512,192]{0,1:T(8,128)}, u32[]{:S(2)}) copy-start(f32[512,192]{0,1:T(8,128)} %get-tuple-element.34) | copy-start | bytes 1179652
where the time goes:
time: 200 us; the launch traced here: 199 us
  blocking collectives  118 us (59%)
  starting transfers between devices  32.3 us (16%)
  waiting for transfers between devices  18.9 us (9%)
  local copies, waits for them, and re-layouts  17.4 us (9%)
  matrix products  9.63 us (5%)
  other arithmetic  2.44 us (1%)
    psum x2, blocking collectives, body(): vertex = lax.psum(spread, ('sub', 'grp'))  86.7 us
    ppermute x20, starting transfers between devices, passed_along(): return lax.ppermute(value, axis, pairs)  23.8 us
    ppermute x20, waiting for transfers between devices, passed_along(): return lax.ppermute(value, axis, pairs)  15.9 us
    all_gather x2, blocking collectives, body(): lax.all_gather(trace_b, 'grp', axis=0, tiled=True)  15.4 us
    all_to_all x1, blocking collectives, body(): lax.all_to_all(coeffs, 'grp', split_axis=2, concat_axis=0, tiled=True)  7.97 us
    all_to_all x1, blocking collectives, body(): lax.all_to_all(own_back.reshape(all_faces, MODES, part_rhs), 'grp', split...  7.64 us
    all_to_all x1, starting transfers between devices, body(): lax.all_to_all(coeffs, 'grp', split_axis=2, concat_axis=0, tiled=True)  4.28 us
    all_to_all x1, starting transfers between devices, body(): lax.all_to_all(own_back.reshape(all_faces, MODES, part_rhs), 'grp', split...  4.26 us
  transfers between devices with their start and end apart: 22, of which 6 were waited for; matrix products, arithmetic and copies ran while one was open for 3% of the time, Pallas kernels for 0%

commit v1 on v0

--- a/solution.py
+++ b/solution.py
@@ -137,7 +137,7 @@
         ).reshape(own_rows, -1)
         partial_value = jnp.dot(coarse_wide, lifted, precision=highest)
         spread = lax.dot_general(corner_hot, partial_value, contract_first, precision=highest)
-        vertex = lax.psum(spread, ("sub", "grp"))
+        vertex = lax.psum(lax.psum(spread, "grp"), "sub")
         picked = jnp.dot(corner_hot, vertex, precision=highest)
         coarse_corr = lax.dot_general(coarse_wide, picked, contract_first, precision=highest)
         traces = traces - relax_weight * lifted - coarse_weight * coarse_corr

time: 200 us -> 209 us (1.045)
  the two profiles are of different devices: /device:TPU:10 before, /device:TPU:0 now
where the time goes in v1:
time: 209 us
  blocking collectives  119 us (57%)
  starting transfers between devices  35.4 us (17%)
  waiting for transfers between devices  23.4 us (11%)
  local copies, waits for them, and re-layouts  17.4 us (8%)
  matrix products  9.64 us (5%)
  other arithmetic  2.46 us (1%)
    psum x4, blocking collectives, body(): vertex = lax.psum(lax.psum(spread, 'grp'), 'sub')  86.2 us
    ppermute x20, starting transfers between devices, passed_along(): return lax.ppermute(value, axis, pairs)  28.7 us
    ppermute x20, waiting for transfers between devices, passed_along(): return lax.ppermute(value, axis, pairs)  18.1 us
    all_gather x2, blocking collectives, body(): lax.all_gather(trace_b, 'grp', axis=0, tiled=True)  17.9 us
    all_to_all x1, blocking collectives, body(): lax.all_to_all(coeffs, 'grp', split_axis=2, concat_axis=0, tiled=True)  7.67 us
    all_to_all x1, blocking collectives, body(): lax.all_to_all(own_back.reshape(all_faces, MODES, part_rhs), 'grp', split...  7.67 us
    all_to_all x1, waiting for transfers between devices, body(): lax.all_to_all(own_back.reshape(all_faces, MODES, part_rhs), 'grp', split...  4.46 us
  transfers between devices with their start and end apart: 22, of which 8 were waited for; matrix products, arithmetic and copies ran while one was open for 3% of the time, Pallas kernels for 0%

profile of v1, /device:TPU:0, one launch (start us, length us, event | category | flops | bytes accessed | tf_op | source)
XLA Modules:
  0.0 208.6 jit_solution(8793378378266768691)
XLA Ops:
  0.0 1.2 reshape_squeeze.3
  1.2 1.0 bitcast_convert_fusion
  2.2 10.1 %all_gather.6 = bf16[2048,192]{0,1:T(8,128)(2,1)S(1)} all-gather(bf16[512,192]{0,1:T(8,128)(2,1)S(1)} %bitcast_convert_fusion), channel_id=1, replica_groups=mesh['sub'=8,'grp'=4] {'grp'}, dimensions={0}, use_global_device_ids=true | all-gather | bytes 983040 | tf_op jit(solution)/shard_map/all_gather | solution.py:94
  12.3 1.8 fusion.20
  14.8 1.0 reshape.310
  15.8 3.4 %all-to-all-start = ((bf16[4,2,12288]{2,1,0:T(2,128)(2,1)}), bf16[4,2,12288]{2,1,0:T(2,128)(2,1)S(1)}, u32[]{:S(2)}, u32[]{:S(2)}) async-start(bf16[4,2,12288]{2,1,0:T(2,128)(2,1)} %reshape.310), calls=%async_computation | async-start | bytes 393216 | tf_op jit(solution)/shard_map/all_to_all | solution.py:102
  19.3 0.6 gather_fusion.3
  19.8 0.6 gather_fusion.1
  20.5 0.3 convert_reduce_fusion
  20.8 0.6 gather_fusion.5
  21.3 0.6 gather_fusion.2
  21.9 0.6 gather_fusion.4
  22.5 0.7 fusion.62
  23.5 0.9 all-to-all-done
  24.4 0.3 reshape.311
  24.7 0.3 copy.70
  25.0 0.8 reshape.235
  26.1 3.6 %collective-permute-start = (bf16[8,3072]{1,0:T(8,128)(2,1)S(1)}, bf16[8,3072]{1,0:T(8,128)(2,1)S(1)}, u32[]{:S(2)}, u32[]{:S(2)}) collective-permute-start(bf16[8,3072]{1,0:T(8,128)(2,1)S(1)} %get-tuple-element.28), channel_id=1, source_target_pairs={{0,24},{4,28},{8,0},{12,4},{16,8},{20,12},{24,16},{28,20},{1,25},{... | collective-permute-start | bytes 147464 | tf_op jit(solution)/shard_map/ppermute | solution.py:20
  29.9 1.6 collective-permute-start.3
  31.4 3.3 %collective-permute-start.1 = (bf16[8,3072]{1,0:T(8,128)(2,1)S(1)}, bf16[8,3072]{1,0:T(8,128)(2,1)S(1)}, u32[]{:S(2)}, u32[]{:S(2)}) collective-permute-start(bf16[8,3072]{1,0:T(8,128)(2,1)S(1)} %get-tuple-element.27), channel_id=1, source_target_pairs={{0,28},{4,0},{8,4},{12,8},{16,12},{20,16},{24,20},{28,24},{1,29},{... | collective-permute-start | bytes 147464 | tf_op jit(solution)/shard_map/ppermute | solution.py:20
  34.7 1.7 collective-permute-done.1
  36.5 0.8 collective-permute-done.3
  37.3 0.7 dot_general.91
  38.0 0.3 copy.72
  38.8 0.3 convert_element_type.96
  39.5 0.6 gather_fusion
  40.0 3.9 %collective-permute-start.9 = (bf16[8,3072]{1,0:T(8,128)(2,1)S(1)}, bf16[8,3072]{1,0:T(8,128)(2,1)S(1)}, u32[]{:S(2)}, u32[]{:S(2)}) collective-permute-start(bf16[8,3072]{1,0:T(8,128)(2,1)S(1)} %get-tuple-element.19), channel_id=1, source_target_pairs={{0,24},{4,28},{8,0},{12,4},{16,8},{20,12},{24,16},{28,20},{1,25},{... | collective-permute-start | bytes 147464 | tf_op jit(solution)/shard_map/ppermute | solution.py:20
  43.9 2.5 %collective-permute-start.8 = (bf16[8,3072]{1,0:T(8,128)(2,1)S(1)}, bf16[8,3072]{1,0:T(8,128)(2,1)S(1)}, u32[]{:S(2)}, u32[]{:S(2)}) collective-permute-start(bf16[8,3072]{1,0:T(8,128)(2,1)S(1)} %get-tuple-element.20), channel_id=1, source_target_pairs={{0,28},{4,0},{8,4},{12,8},{16,12},{20,16},{24,20},{28,24},{1,29},{... | collective-permute-start | bytes 147464 | tf_op jit(solution)/shard_map/ppermute | solution.py:20
  46.4 6.8 %collective-permute-done.6 = bf16[8,3072]{1,0:T(8,128)(2,1)S(1)} collective-permute-done((bf16[8,3072]{1,0:T(8,128)(2,1)S(1)}, bf16[8,3072]{1,0:T(8,128)(2,1)S(1)}, u32[]{:S(2)}, u32[]{:S(2)}) %collective-permute-start.6) | collective-permute-done | bytes 49184 | tf_op jit(solution)/shard_map/ppermute | solution.py:20
  53.5 0.5 reshape.236
  54.3 1.0 reshape.312
  55.3 3.4 %all-to-all-start.1 = ((bf16[4,2,12288]{2,1,0:T(2,128)(2,1)}), bf16[4,2,12288]{2,1,0:T(2,128)(2,1)S(1)}, u32[]{:S(2)}, u32[]{:S(2)}) async-start(bf16[4,2,12288]{2,1,0:T(2,128)(2,1)} %reshape.312), calls=%async_computation.1 | async-start | bytes 393216 | tf_op jit(solution)/shard_map/all_to_all | solution.py:128
  58.7 0.8 broadcast_select_fusion.4
  59.5 4.5 %all-to-all-done.1 = bf16[4,2,12288]{2,1,0:T(2,128)(2,1)S(1)} async-done(((bf16[4,2,12288]{2,1,0:T(2,128)(2,1)}), bf16[4,2,12288]{2,1,0:T(2,128)(2,1)S(1)}, u32[]{:S(2)}, u32[]{:S(2)}) %all-to-all-start.1) | async-done | bytes 196640 | tf_op jit(solution)/shard_map/all_to_all | solution.py:128
  64.0 0.3 reshape.313
  64.3 0.4 fusion.73
  65.1 0.3 fusion.55
  65.4 10.1 %psum.28 = f32[16,192]{1,0:T(8,128)S(1)} all-reduce(f32[16,192]{1,0:T(8,128)S(1)} %fusion.55), channel_id=1, replica_groups=mesh['sub'=8,'grp'=4] {'grp'}, use_global_device_ids=true, to_apply=%region_1.0 | all-reduce | flops 3072 | bytes 24576 | tf_op jit(solution)/shard_map/psum | solution.py:140
  75.5 33.0 %psum.29 = f32[16,192]{1,0:T(8,128)S(1)} all-reduce(f32[16,192]{1,0:T(8,128)S(1)} %psum.28), channel_id=1, replica_groups=mesh['sub'=8,'grp'=4] {'sub'}, use_global_device_ids=true, to_apply=%region_2.5 | all-reduce | flops 3072 | bytes 24576 | tf_op jit(solution)/shard_map/psum | solution.py:140
  108.7 1.1 fusion.72
  109.8 7.9 %all_gather.7 = bf16[2048,192]{0,1:T(8,128)(2,1)S(1)} all-gather(bf16[512,192]{0,1:T(8,128)(2,1)S(1)} %get-tuple-element.33), channel_id=1, replica_groups=mesh['sub'=8,'grp'=4] {'grp'}, dimensions={0}, use_global_device_ids=true | all-gather | bytes 983040 | tf_op jit(solution)/shard_map/all_gather | solution.py:94
  117.7 0.8 fusion.23
  119.2 0.3 reshape.314
  119.5 7.7 %all_to_all.66 = bf16[4,2,12288]{2,1,0:T(2,128)(2,1)S(1)} all-to-all(bf16[4,2,12288]{2,1,0:T(2,128)(2,1)S(1)} %reshape.314), channel_id=1, replica_groups=mesh['sub'=8,'grp'=4] {'grp'}, dimensions={0} | all-to-all | bytes 393216 | tf_op jit(solution)/shard_map/all_to_all | solution.py:102
  127.2 0.3 reshape.315
  127.5 0.3 copy.82
  127.8 0.8 reshape.239
  128.9 2.0 collective-permute-start.14
  130.9 4.7 %collective-permute-start.11 = (bf16[8,3072]{1,0:T(8,128)(2,1)S(1)}, bf16[8,3072]{1,0:T(8,128)(2,1)S(1)}, u32[]{:S(2)}, u32[]{:S(2)}) collective-permute-start(bf16[8,3072]{1,0:T(8,128)(2,1)S(1)} %get-tuple-element.17), channel_id=1, source_target_pairs={{0,28},{4,0},{8,4},{12,8},{16,12},{20,16},{24,20},{28,24},{1,29},{... | collective-permute-start | bytes 147464 | tf_op jit(solution)/shard_map/ppermute | solution.py:20
  135.7 1.7 collective-permute-done.11
  137.4 0.3 collective-permute-done.13
  137.7 0.7 dot_general.107
  138.4 0.3 copy.84
  139.3 0.3 convert_element_type.105
  139.9 3.8 %collective-permute-start.19 = (bf16[8,3072]{1,0:T(8,128)(2,1)S(1)}, bf16[8,3072]{1,0:T(8,128)(2,1)S(1)}, u32[]{:S(2)}, u32[]{:S(2)}) collective-permute-start(bf16[8,3072]{1,0:T(8,128)(2,1)S(1)} %get-tuple-element.9), channel_id=1, source_target_pairs={{0,24},{4,28},{8,0},{12,4},{16,8},{20,12},{24,16},{28,20},{1,25},{... | collective-permute-start | bytes 147464 | tf_op jit(solution)/shard_map/ppermute | solution.py:20
  143.7 3.1 %collective-permute-start.18 = (bf16[8,3072]{1,0:T(8,128)(2,1)S(1)}, bf16[8,3072]{1,0:T(8,128)(2,1)S(1)}, u32[]{:S(2)}, u32[]{:S(2)}) collective-permute-start(bf16[8,3072]{1,0:T(8,128)(2,1)S(1)} %get-tuple-element.10), channel_id=1, source_target_pairs={{0,28},{4,0},{8,4},{12,8},{16,12},{20,16},{24,20},{28,24},{1,29},{... | collective-permute-start | bytes 147464 | tf_op jit(solution)/shard_map/ppermute | solution.py:20
  146.9 6.8 %collective-permute-done.16 = bf16[8,3072]{1,0:T(8,128)(2,1)S(1)} collective-permute-done((bf16[8,3072]{1,0:T(8,128)(2,1)S(1)}, bf16[8,3072]{1,0:T(8,128)(2,1)S(1)}, u32[]{:S(2)}, u32[]{:S(2)}) %collective-permute-start.16) | collective-permute-done | bytes 49184 | tf_op jit(solution)/shard_map/ppermute | solution.py:20
  154.0 0.5 reshape.240
  154.8 0.3 reshape.316
  155.1 7.7 %all_to_all.67 = bf16[4,2,12288]{2,1,0:T(2,128)(2,1)S(1)} all-to-all(bf16[4,2,12288]{2,1,0:T(2,128)(2,1)S(1)} %reshape.316), channel_id=1, replica_groups=mesh['sub'=8,'grp'=4] {'grp'}, dimensions={0} | all-to-all | bytes 393216 | tf_op jit(solution)/shard_map/all_to_all | solution.py:128
  163.1 0.4 fusion.74
  164.2 10.1 %psum.30 = f32[16,192]{1,0:T(8,128)S(1)} all-reduce(f32[16,192]{1,0:T(8,128)S(1)} %fusion.53), channel_id=1, replica_groups=mesh['sub'=8,'grp'=4] {'grp'}, use_global_device_ids=true, to_apply=%region_3.6 | all-reduce | flops 3072 | bytes 24576 | tf_op jit(solution)/shard_map/psum | solution.py:140
  174.3 33.0 %psum.31 = f32[16,192]{1,0:T(8,128)S(1)} all-reduce(f32[16,192]{1,0:T(8,128)S(1)} %psum.30), channel_id=1, replica_groups=mesh['sub'=8,'grp'=4] {'sub'}, use_global_device_ids=true, to_apply=%region_4.7 | all-reduce | flops 3072 | bytes 24576 | tf_op jit(solution)/shard_map/psum | solution.py:140
  207.5 1.1 fusion.6
  (124 shorter events, 7.0 us)
Async XLA Ops:
  0.0 12.3 %copy-start = (bf16[1,512,2048]{2,1,0:T(8,128)(2,1)S(1)}, bf16[1,512,2048]{2,1,0:T(8,128)(2,1)}, u32[]{:S(2)}) copy-start(bf16[1,512,2048]{2,1,0:T(8,128)(2,1)} %param.14) | copy-start | bytes 6291460
  14.1 5.0 %copy-start.13 = (s32[8]{0:T(128)S(1)}, s32[8]{0:T(128)}, u32[]{:S(2)}) copy-start(s32[8]{0:T(128)} %param.22) | copy-start | bytes 100
  14.1 5.1 %copy-start.4 = (s32[8,32]{1,0:T(8,128)S(1)}, s32[8,32]{1,0:T(8,128)}, u32[]{:S(2)}) copy-start(s32[8,32]{1,0:T(8,128)} %param.20) | copy-start | bytes 3076
  14.2 5.7 %copy-start.5 = (s32[8,32,1]{1,2,0:T(1,128)S(1)}, s32[8,32,1]{1,2,0:T(1,128)}, u32[]{:S(2)}) copy-start(s32[8,32,1]{1,2,0:T(1,128)} %param.19) | copy-start | bytes 3076
  15.8 8.6 %all-to-all-start = ((bf16[4,2,12288]{2,1,0:T(2,128)(2,1)}), bf16[4,2,12288]{2,1,0:T(2,128)(2,1)S(1)}, u32[]{:S(2)}, u32[]{:S(2)}) async-start(bf16[4,2,12288]{2,1,0:T(2,128)(2,1)} %reshape.310), calls=%async_computation | async-start | bytes 393216 | tf_op jit(solution)/shard_map/all_to_all | solution.py:102
  19.2 5.5 %copy-start.12 = (pred[8]{0:T(512)(128)(4,1)}, pred[8]{0:T(512)(128)(4,1)S(1)}, u32[]{:S(2)}) copy-start(pred[8]{0:T(512)(128)(4,1)S(1)} %compare_and_fusion.1) | copy-start | bytes 28
  23.4 15.7 %copy-start.8 = (bf16[5,8,16]{2,1,0:T(8,128)(2,1)}, bf16[5,8,16]{2,1,0:T(8,128)(2,1)S(1)}, u32[]{:S(2)}) copy-start(bf16[5,8,16]{2,1,0:T(8,128)(2,1)S(1)} %convolution_convert_fusion.8) | copy-start | bytes 3844
  23.5 14.8 %copy-start.10 = (f32[16,64]{1,0:T(8,128)}, f32[16,64]{1,0:T(8,128)S(1)}, u32[]{:S(2)}) copy-start(f32[16,64]{1,0:T(8,128)S(1)} %and_convert_fusion) | copy-start | bytes 12292
  26.1 8.6 %collective-permute-start = (bf16[8,3072]{1,0:T(8,128)(2,1)S(1)}, bf16[8,3072]{1,0:T(8,128)(2,1)S(1)}, u32[]{:S(2)}, u32[]{:S(2)}) collective-permute-start(bf16[8,3072]{1,0:T(8,128)(2,1)S(1)} %get-tuple-element.28), channel_id=1, source_target_pairs={{0,24},{4,28},{8,0},{12,4},{16,8},{20,12},{24,16},{28,20},{1,25},{... | collective-permute-start | bytes 147464 | tf_op jit(solution)/shard_map/ppermute | solution.py:20
  29.9 9.0 %copy-start.14 = (f32[16]{0:T(128)}, f32[16]{0:T(128)S(1)}, u32[]{:S(2)}) copy-start(f32[16]{0:T(128)S(1)} %fusion.30) | copy-start | bytes 196
  29.9 7.4 %collective-permute-start.4 = (bf16[8,3072]{1,0:T(8,128)(2,1)S(1)}, bf16[8,3072]{1,0:T(8,128)(2,1)S(1)}, u32[]{:S(2)}, u32[]{:S(2)}) collective-permute-start(bf16[8,3072]{1,0:T(8,128)(2,1)S(1)} %get-tuple-element.24), channel_id=1, source_target_pairs={{0,8},{4,12},{8,16},{12,20},{16,24},{20,28},{24,0},{28,4},{1,9},{5... | collective-permute-start | bytes 147464 | tf_op jit(solution)/shard_map/ppermute | solution.py:20
  29.9 7.4 %collective-permute-start.3 = (bf16[8,3072]{1,0:T(8,128)(2,1)S(1)}, bf16[8,3072]{1,0:T(8,128)(2,1)S(1)}, u32[]{:S(2)}, u32[]{:S(2)}) collective-permute-start(bf16[8,3072]{1,0:T(8,128)(2,1)S(1)} %get-tuple-element.25), channel_id=1, source_target_pairs={{0,4},{4,8},{8,12},{12,16},{16,20},{20,24},{24,28},{28,0},{1,5},{5... | collective-permute-start | bytes 147464 | tf_op jit(solution)/shard_map/ppermute | solution.py:20
  31.4 5.1 %collective-permute-start.2 = (bf16[8,3072]{1,0:T(8,128)(2,1)S(1)}, bf16[8,3072]{1,0:T(8,128)(2,1)S(1)}, u32[]{:S(2)}, u32[]{:S(2)}) collective-permute-start(bf16[8,3072]{1,0:T(8,128)(2,1)S(1)} %get-tuple-element.26), channel_id=1, source_target_pairs={{0,0},{4,4},{8,8},{12,12},{16,16},{20,20},{24,24},{28,28},{1,1},{5... | collective-permute-start | bytes 147464 | tf_op jit(solution)/shard_map/ppermute | solution.py:20
  31.4 5.0 %collective-permute-start.1 = (bf16[8,3072]{1,0:T(8,128)(2,1)S(1)}, bf16[8,3072]{1,0:T(8,128)(2,1)S(1)}, u32[]{:S(2)}, u32[]{:S(2)}) collective-permute-start(bf16[8,3072]{1,0:T(8,128)(2,1)S(1)} %get-tuple-element.27), channel_id=1, source_target_pairs={{0,28},{4,0},{8,4},{12,8},{16,12},{20,16},{24,20},{28,24},{1,29},{... | collective-permute-start | bytes 147464 | tf_op jit(solution)/shard_map/ppermute | solution.py:20
  37.9 1.5 copy-start.6
  39.4 7.0 %collective-permute-start.5 = (bf16[8,3072]{1,0:T(8,128)(2,1)S(1)}, bf16[8,3072]{1,0:T(8,128)(2,1)S(1)}, u32[]{:S(2)}, u32[]{:S(2)}) collective-permute-start(bf16[8,3072]{1,0:T(8,128)(2,1)S(1)} %get-tuple-element.23), channel_id=1, source_target_pairs={{0,8},{4,12},{8,16},{12,20},{16,24},{20,28},{24,0},{28,4},{1,9},{5... | collective-permute-start | bytes 147464 | tf_op jit(solution)/shard_map/ppermute | solution.py:20
  40.0 13.2 %collective-permute-start.9 = (bf16[8,3072]{1,0:T(8,128)(2,1)S(1)}, bf16[8,3072]{1,0:T(8,128)(2,1)S(1)}, u32[]{:S(2)}, u32[]{:S(2)}) collective-permute-start(bf16[8,3072]{1,0:T(8,128)(2,1)S(1)} %get-tuple-element.19), channel_id=1, source_target_pairs={{0,24},{4,28},{8,0},{12,4},{16,8},{20,12},{24,16},{28,20},{1,25},{... | collective-permute-start | bytes 147464 | tf_op jit(solution)/shard_map/ppermute | solution.py:20
  43.9 9.3 %collective-permute-start.8 = (bf16[8,3072]{1,0:T(8,128)(2,1)S(1)}, bf16[8,3072]{1,0:T(8,128)(2,1)S(1)}, u32[]{:S(2)}, u32[]{:S(2)}) collective-permute-start(bf16[8,3072]{1,0:T(8,128)(2,1)S(1)} %get-tuple-element.20), channel_id=1, source_target_pairs={{0,28},{4,0},{8,4},{12,8},{16,12},{20,16},{24,20},{28,24},{1,29},{... | collective-permute-start | bytes 147464 | tf_op jit(solution)/shard_map/ppermute | solution.py:20
  46.4 6.8 %collective-permute-start.7 = (bf16[8,3072]{1,0:T(8,128)(2,1)S(1)}, bf16[8,3072]{1,0:T(8,128)(2,1)S(1)}, u32[]{:S(2)}, u32[]{:S(2)}) collective-permute-start(bf16[8,3072]{1,0:T(8,128)(2,1)S(1)} %get-tuple-element.21), channel_id=1, source_target_pairs={{0,0},{4,4},{8,8},{12,12},{16,16},{20,20},{24,24},{28,28},{1,1},{5... | collective-permute-start | bytes 147464 | tf_op jit(solution)/shard_map/ppermute | solution.py:20
  46.4 6.8 %collective-permute-start.6 = (bf16[8,3072]{1,0:T(8,128)(2,1)S(1)}, bf16[8,3072]{1,0:T(8,128)(2,1)S(1)}, u32[]{:S(2)}, u32[]{:S(2)}) collective-permute-start(bf16[8,3072]{1,0:T(8,128)(2,1)S(1)} %get-tuple-element.22), channel_id=1, source_target_pairs={{0,4},{4,8},{8,12},{12,16},{16,20},{20,24},{24,28},{28,0},{1,5},{5... | collective-permute-start | bytes 147464 | tf_op jit(solution)/shard_map/ppermute | solution.py:20
  54.3 10.6 %copy-start.7 = (bf16[1,8,512]{2,1,0:T(8,128)(2,1)S(1)}, bf16[1,8,512]{2,1,0:T(8,128)(2,1)}, u32[]{:S(2)}) copy-start(bf16[1,8,512]{2,1,0:T(8,128)(2,1)} %param.18) | copy-start | bytes 24580
  55.3 8.6 %all-to-all-start.1 = ((bf16[4,2,12288]{2,1,0:T(2,128)(2,1)}), bf16[4,2,12288]{2,1,0:T(2,128)(2,1)S(1)}, u32[]{:S(2)}, u32[]{:S(2)}) async-start(bf16[4,2,12288]{2,1,0:T(2,128)(2,1)} %reshape.312), calls=%async_computation.1 | async-start | bytes 393216 | tf_op jit(solution)/shard_map/all_to_all | solution.py:128
  58.7 50.0 %copy-start.1 = (f32[1,512,192]{1,2,0:T(8,128)S(1)}, f32[1,512,192]{1,2,0:T(8,128)}, u32[]{:S(2)}) copy-start(f32[1,512,192]{1,2,0:T(8,128)} %param.16) | copy-start | bytes 1179652
  108.5 9.2 %copy-start.3 = (f32[1,512,192]{1,2,0:T(8,128)S(1)}, f32[1,512,192]{1,2,0:T(8,128)}, u32[]{:S(2)}) copy-start(f32[1,512,192]{1,2,0:T(8,128)} %param.15) | copy-start | bytes 1179652
  127.8 11.0 %copy-start.9 = (bf16[5,8,16]{2,1,0:T(8,128)(2,1)S(1)}, bf16[5,8,16]{2,1,0:T(8,128)(2,1)}, u32[]{:S(2)}) copy-start(bf16[5,8,16]{2,1,0:T(8,128)(2,1)} %copy-done.8) | copy-start | bytes 3844
  127.8 11.0 %copy-start.11 = (f32[16,64]{1,0:T(8,128)S(1)}, f32[16,64]{1,0:T(8,128)}, u32[]{:S(2)}) copy-start(f32[16,64]{1,0:T(8,128)} %copy-done.10) | copy-start | bytes 12292
  127.8 11.0 %copy-start.15 = (f32[16]{0:T(128)S(1)}, f32[16]{0:T(128)}, u32[]{:S(2)}) copy-start(f32[16]{0:T(128)} %copy-done.14) | copy-start | bytes 196
  128.8 6.8 %collective-permute-start.10 = (bf16[8,3072]{1,0:T(8,128)(2,1)S(1)}, bf16[8,3072]{1,0:T(8,128)(2,1)S(1)}, u32[]{:S(2)}, u32[]{:S(2)}) collective-permute-start(bf16[8,3072]{1,0:T(8,128)(2,1)S(1)} %get-tuple-element.18), channel_id=1, source_target_pairs={{0,24},{4,28},{8,0},{12,4},{16,8},{20,12},{24,16},{28,20},{1,25},{... | collective-permute-start | bytes 147464 | tf_op jit(solution)/shard_map/ppermute | solution.py:20
  128.9 8.8 %collective-permute-start.14 = (bf16[8,3072]{1,0:T(8,128)(2,1)S(1)}, bf16[8,3072]{1,0:T(8,128)(2,1)S(1)}, u32[]{:S(2)}, u32[]{:S(2)}) collective-permute-start(bf16[8,3072]{1,0:T(8,128)(2,1)S(1)} %get-tuple-element.14), channel_id=1, source_target_pairs={{0,8},{4,12},{8,16},{12,20},{16,24},{20,28},{24,0},{28,4},{1,9},{5... | collective-permute-start | bytes 147464 | tf_op jit(solution)/shard_map/ppermute | solution.py:20
  130.9 6.8 %collective-permute-start.13 = (bf16[8,3072]{1,0:T(8,128)(2,1)S(1)}, bf16[8,3072]{1,0:T(8,128)(2,1)S(1)}, u32[]{:S(2)}, u32[]{:S(2)}) collective-permute-start(bf16[8,3072]{1,0:T(8,128)(2,1)S(1)} %get-tuple-element.15), channel_id=1, source_target_pairs={{0,4},{4,8},{8,12},{12,16},{16,20},{20,24},{24,28},{28,0},{1,5},{5... | collective-permute-start | bytes 147464 | tf_op jit(solution)/shard_map/ppermute | solution.py:20
  130.9 6.5 %collective-permute-start.12 = (bf16[8,3072]{1,0:T(8,128)(2,1)S(1)}, bf16[8,3072]{1,0:T(8,128)(2,1)S(1)}, u32[]{:S(2)}, u32[]{:S(2)}) collective-permute-start(bf16[8,3072]{1,0:T(8,128)(2,1)S(1)} %get-tuple-element.16), channel_id=1, source_target_pairs={{0,0},{4,4},{8,8},{12,12},{16,16},{20,20},{24,24},{28,28},{1,1},{5... | collective-permute-start | bytes 147464 | tf_op jit(solution)/shard_map/ppermute | solution.py:20
  130.9 6.5 %collective-permute-start.11 = (bf16[8,3072]{1,0:T(8,128)(2,1)S(1)}, bf16[8,3072]{1,0:T(8,128)(2,1)S(1)}, u32[]{:S(2)}, u32[]{:S(2)}) collective-permute-start(bf16[8,3072]{1,0:T(8,128)(2,1)S(1)} %get-tuple-element.17), channel_id=1, source_target_pairs={{0,28},{4,0},{8,4},{12,8},{16,12},{20,16},{24,20},{28,24},{1,29},{... | collective-permute-start | bytes 147464 | tf_op jit(solution)/shard_map/ppermute | solution.py:20
  139.9 7.0 %collective-permute-start.15 = (bf16[8,3072]{1,0:T(8,128)(2,1)S(1)}, bf16[8,3072]{1,0:T(8,128)(2,1)S(1)}, u32[]{:S(2)}, u32[]{:S(2)}) collective-permute-start(bf16[8,3072]{1,0:T(8,128)(2,1)S(1)} %get-tuple-element.13), channel_id=1, source_target_pairs={{0,8},{4,12},{8,16},{12,20},{16,24},{20,28},{24,0},{28,4},{1,9},{5... | collective-permute-start | bytes 147464 | tf_op jit(solution)/shard_map/ppermute | solution.py:20
  139.9 13.7 %collective-permute-start.19 = (bf16[8,3072]{1,0:T(8,128)(2,1)S(1)}, bf16[8,3072]{1,0:T(8,128)(2,1)S(1)}, u32[]{:S(2)}, u32[]{:S(2)}) collective-permute-start(bf16[8,3072]{1,0:T(8,128)(2,1)S(1)} %get-tuple-element.9), channel_id=1, source_target_pairs={{0,24},{4,28},{8,0},{12,4},{16,8},{20,12},{24,16},{28,20},{1,25},{... | collective-permute-start | bytes 147464 | tf_op jit(solution)/shard_map/ppermute | solution.py:20
  143.7 9.9 %collective-permute-start.18 = (bf16[8,3072]{1,0:T(8,128)(2,1)S(1)}, bf16[8,3072]{1,0:T(8,128)(2,1)S(1)}, u32[]{:S(2)}, u32[]{:S(2)}) collective-permute-start(bf16[8,3072]{1,0:T(8,128)(2,1)S(1)} %get-tuple-element.10), channel_id=1, source_target_pairs={{0,28},{4,0},{8,4},{12,8},{16,12},{20,16},{24,20},{28,24},{1,29},{... | collective-permute-start | bytes 147464 | tf_op jit(solution)/shard_map/ppermute | solution.py:20
  146.8 6.8 %collective-permute-start.17 = (bf16[8,3072]{1,0:T(8,128)(2,1)S(1)}, bf16[8,3072]{1,0:T(8,128)(2,1)S(1)}, u32[]{:S(2)}, u32[]{:S(2)}) collective-permute-start(bf16[8,3072]{1,0:T(8,128)(2,1)S(1)} %get-tuple-element.11), channel_id=1, source_target_pairs={{0,0},{4,4},{8,8},{12,12},{16,16},{20,20},{24,24},{28,28},{1,1},{5... | collective-permute-start | bytes 147464 | tf_op jit(solution)/shard_map/ppermute | solution.py:20
  146.8 6.8 %collective-permute-start.16 = (bf16[8,3072]{1,0:T(8,128)(2,1)S(1)}, bf16[8,3072]{1,0:T(8,128)(2,1)S(1)}, u32[]{:S(2)}, u32[]{:S(2)}) collective-permute-start(bf16[8,3072]{1,0:T(8,128)(2,1)S(1)} %get-tuple-element.12), channel_id=1, source_target_pairs={{0,4},{4,8},{8,12},{12,16},{16,20},{20,24},{24,28},{28,0},{1,5},{5... | collective-permute-start | bytes 147464 | tf_op jit(solution)/shard_map/ppermute | solution.py:20
  162.7 44.7 %copy-start.2 = (f32[512,192]{0,1:T(8,128)S(1)}, f32[512,192]{0,1:T(8,128)}, u32[]{:S(2)}) copy-start(f32[512,192]{0,1:T(8,128)} %get-tuple-element.34) | copy-start | bytes 1179652
